TPU v7x, 32 devices: a whole 2x2x4 slice. The times are simulated.
32 devices in a mesh: fsdp: 4 (over z), ctx: 2 (over x), tp: 4 (over y, core).
Axes of the slice: x: 2, y: 2, z: 4, core: 2. Of those that a mesh axis runs over, the one named last changes fastest.
Arguments:
- layer_in: bfloat16 [8, 1024, 1024], P('fsdp', ('ctx', 'tp')), may hold values from -6 to 6
- attn_gain: bfloat16 [1024], replicated, may hold values from 0.5 to 1.5
- ffn_gain: bfloat16 [1024], replicated, may hold values from 0.5 to 1.5
- query_weight: bfloat16 [1024, 1024], P(('fsdp', 'ctx'), 'tp'), may hold values from -0.1875 to 0.1875
- key_weight: bfloat16 [1024, 1024], P(('fsdp', 'ctx'), 'tp'), may hold values from -0.1875 to 0.1875
- value_weight: bfloat16 [1024, 1024], P(('fsdp', 'ctx'), 'tp'), may hold values from -0.1875 to 0.1875
- out_weight: bfloat16 [1024, 1024], P(('fsdp', 'ctx'), 'tp'), may hold values from -0.75 to 0.75
- variate_bias: float32 [2, 16], P(None, 'tp'), may hold values from -4 to 4
- gate_weight: bfloat16 [1024, 4096], P(('fsdp', 'ctx'), 'tp'), may hold values from -0.1875 to 0.1875
- up_weight: bfloat16 [1024, 4096], P(('fsdp', 'ctx'), 'tp'), may hold values from -0.1875 to 0.1875
- down_weight: bfloat16 [1024, 4096], P(('fsdp', 'ctx'), 'tp'), may hold values from -0.09375 to 0.09375
- segment_ids: int32 [8, 1024], P('fsdp'), may hold values from 0 to 15, never falling along the last dimension, each value on 1 to 512 neighbouring positions
- variate_ids: int32 [8, 1024], P('fsdp'), may hold values from 0 to 3
- time_ids: int32 [8, 1024], P('fsdp'), may hold values from 0 to 1023
- out_grad: bfloat16 [8, 1024, 1024], P('fsdp', ('ctx', 'tp')), may hold values from -6 to 6
Outputs:
- layer_out: bfloat16 [8, 1024, 1024], P('fsdp', ('ctx', 'tp'))
- in_grad: bfloat16 [8, 1024, 1024], P('fsdp', ('ctx', 'tp'))
- attn_gain_grad: float32 [1024], replicated
- ffn_gain_grad: float32 [1024], replicated
- query_grad: float32 [1024, 1024], P(('fsdp', 'ctx'), 'tp')
- key_grad: float32 [1024, 1024], P(('fsdp', 'ctx'), 'tp')
- value_grad: float32 [1024, 1024], P(('fsdp', 'ctx'), 'tp')
- out_weight_grad: float32 [1024, 1024], P(('fsdp', 'ctx'), 'tp')
- bias_grad: float32 [2, 16], P(None, 'tp')
- gate_grad: float32 [1024, 4096], P(('fsdp', 'ctx'), 'tp')
- up_grad: float32 [1024, 4096], P(('fsdp', 'ctx'), 'tp')
- down_grad: float32 [1024, 4096], P(('fsdp', 'ctx'), 'tp')
All inputs are finite; a program needn't handle non-finite values.
Results may differ from a plain program's by a relative error of at most 0.019.
Values may be sent and summed in bfloat16 or wider, within the bound.
No kernel may reach another device: no remote copies, remote signals or barrier semaphores. Data moves between devices by JAX's collectives and lax.ppermute only.
A program may use at most 128 MiB of HBM per device.

v0:
```python
import jax
import jax.numpy as jnp
from jax import lax
from jax.sharding import PartitionSpec as P

HEADS = 16
HEAD = 64
EPS = 1e-05
NEG = -1e30


def rms_norm(values, gain):
    return values * lax.rsqrt(jnp.mean(values * values, axis=-1, keepdims=True) + EPS) * gain


def rotate(values, time_rows):
    half_dim = values.shape[-1] // 2
    frequency = 10000.0 ** (-2.0 * jnp.arange(half_dim, dtype=jnp.float32) / values.shape[-1])
    angles = time_rows.astype(jnp.float32)[..., None, None] * frequency
    cosine = jnp.cos(angles)
    sine_part = jnp.sin(angles)
    first_half = values[..., :half_dim]
    second = values[..., half_dim:]
    return jnp.concatenate(
        [first_half * cosine - second * sine_part, second * cosine + first_half * sine_part],
        axis=-1,
    )


def swiglu(gate_vals, up_vals):
    return jax.nn.silu(gate_vals) * up_vals


def gather_rows(values):
    return lax.all_gather(values, "tp", axis=1, tiled=True)


def scatter_rows(values):
    return lax.psum_scatter(values, "tp", scatter_dimension=1, tiled=True)


def shards(
    layer_in,
    attn_gain,
    ffn_gain,
    query_weight,
    key_weight,
    value_weight,
    out_weight,
    variate_bias,
    gate_weight,
    up_weight,
    down_weight,
    segment_ids,
    variate_ids,
    time_ids,
    out_grad,
):
    seq_count, share, width = layer_in.shape
    span = share * lax.axis_size("tp")
    seq_length = segment_ids.shape[1]
    offset = lax.axis_index("ctx") * span
    local_heads = variate_bias.shape[1]
    proj_width = local_heads * HEAD
    row_count = seq_count * span
    block = 512
    block_starts = jnp.arange(span // block, dtype=jnp.int32) * block
    scale = HEAD ** (-0.5)
    my_times = lax.dynamic_slice_in_dim(time_ids, offset, span, 1)
    my_variates = lax.dynamic_slice_in_dim(variate_ids, offset, span, 1)
    my_segments = lax.dynamic_slice_in_dim(segment_ids, offset, span, 1)
    bias_same = variate_bias[0]
    bias_diff = variate_bias[1]
    gain_one = attn_gain.astype(jnp.float32)
    gain_two = ffn_gain.astype(jnp.float32)
    inputs = layer_in.astype(jnp.float32)
    rows_one = gather_rows(rms_norm(inputs, gain_one).astype(jnp.bfloat16)).reshape(
        row_count, width
    )
    query_full, key_full, value_full, out_full = (
        lax.all_gather(query_weight, ("fsdp", "ctx"), axis=0, tiled=True),
        lax.all_gather(key_weight, ("fsdp", "ctx"), axis=0, tiled=True),
        lax.all_gather(value_weight, ("fsdp", "ctx"), axis=0, tiled=True),
        lax.all_gather(out_weight, ("fsdp", "ctx"), axis=0, tiled=True),
    )
    queries_raw = jnp.dot(rows_one, query_full, preferred_element_type=jnp.float32).reshape(
        seq_count, span, local_heads, HEAD
    )
    keys_raw = jnp.dot(rows_one, key_full, preferred_element_type=jnp.float32).reshape(
        seq_count, span, local_heads, HEAD
    )
    queries = rotate(queries_raw, my_times).astype(jnp.bfloat16)
    keys_mine = rotate(keys_raw, my_times).astype(jnp.bfloat16).reshape(seq_count, span, proj_width)
    values_mine = (
        jnp.dot(rows_one, value_full, preferred_element_type=jnp.float32)
        .astype(jnp.bfloat16)
        .reshape(seq_count, span, proj_width)
    )
    keys_all, values_all = (
        lax.all_gather(keys_mine, "ctx", axis=1, tiled=True),
        lax.all_gather(values_mine, "ctx", axis=1, tiled=True),
    )

    def scores_of(query_block, key_rows, query_var, key_var, query_seg, key_seg):
        raw = (
            jnp.einsum("qhd,khd->hqk", query_block, key_rows, preferred_element_type=jnp.float32)
            * scale
        )
        same = (query_var[:, None] == key_var[None, :])[None]
        raw = raw + jnp.where(same, bias_same[:, None, None], bias_diff[:, None, None])
        return (jnp.where((query_seg[:, None] == key_seg[None, :])[None], raw, NEG), same)

    mixed_parts = []
    lse_parts = []
    for seq in range(seq_count):
        key_rows = keys_all[seq].reshape(seq_length, local_heads, HEAD)
        value_rows = values_all[seq].reshape(seq_length, local_heads, HEAD)

        def forward_block(first, seq=seq, key_rows=key_rows, value_rows=value_rows):
            query_block = queries[seq]
            query_var = my_variates[seq]
            query_seg = my_segments[seq]
            scores, same = scores_of(
                query_block, key_rows, query_var, variate_ids[seq], query_seg, segment_ids[seq]
            )
            top = jnp.max(scores, axis=-1, keepdims=True)
            expo = jnp.exp(scores - top)
            total = jnp.sum(expo, axis=-1, keepdims=True)
            probs = (expo / total).astype(jnp.bfloat16)
            mixed_block = jnp.einsum(
                "hqk,khd->qhd", probs, value_rows, preferred_element_type=jnp.float32
            )
            return (
                mixed_block.astype(jnp.bfloat16).reshape(block, proj_width),
                top[..., 0] + jnp.log(total[..., 0]),
            )

        mixed_seq, lse_seq = lax.map(forward_block, block_starts)
        mixed_parts.append(mixed_seq.reshape(span, proj_width))
        lse_parts.append(lse_seq)
    mixed = jnp.stack(mixed_parts).reshape(row_count, proj_width)
    attn_part = jnp.einsum("rp,dp->rd", mixed, out_full, preferred_element_type=jnp.float32)
    hidden = inputs + scatter_rows(attn_part.reshape(seq_count, span, width))
    rows_two = gather_rows(rms_norm(hidden, gain_two).astype(jnp.bfloat16)).reshape(
        row_count, width
    )
    gate_full, up_full, down_full = (
        lax.all_gather(gate_weight, ("fsdp", "ctx"), axis=0, tiled=True),
        lax.all_gather(up_weight, ("fsdp", "ctx"), axis=0, tiled=True),
        lax.all_gather(down_weight, ("fsdp", "ctx"), axis=0, tiled=True),
    )
    gate = jnp.dot(rows_two, gate_full, preferred_element_type=jnp.float32)
    up_vals = jnp.dot(rows_two, up_full, preferred_element_type=jnp.float32)
    act = swiglu(gate, up_vals).astype(jnp.bfloat16)
    ffn_part = jnp.einsum("rf,df->rd", act, down_full, preferred_element_type=jnp.float32)
    layer_out = (hidden + scatter_rows(ffn_part.reshape(seq_count, span, width))).astype(
        jnp.bfloat16
    )
    query_back, key_back, value_back, out_back = (
        lax.all_gather(query_weight, ("fsdp", "ctx"), axis=0, tiled=True),
        lax.all_gather(key_weight, ("fsdp", "ctx"), axis=0, tiled=True),
        lax.all_gather(value_weight, ("fsdp", "ctx"), axis=0, tiled=True),
        lax.all_gather(out_weight, ("fsdp", "ctx"), axis=0, tiled=True),
    )
    gate_back, up_back, down_back = (
        lax.all_gather(gate_weight, ("fsdp", "ctx"), axis=0, tiled=True),
        lax.all_gather(up_weight, ("fsdp", "ctx"), axis=0, tiled=True),
        lax.all_gather(down_weight, ("fsdp", "ctx"), axis=0, tiled=True),
    )
    grad_rows = gather_rows(out_grad).reshape(row_count, width)
    d_act = jnp.dot(grad_rows, down_back, preferred_element_type=jnp.float32)
    down_local = jnp.einsum("rd,rf->df", grad_rows, act, preferred_element_type=jnp.float32)
    swiglu_pull = jax.vjp(swiglu, gate, up_vals)[1]
    d_gate, d_up = swiglu_pull(d_act)
    d_gate = d_gate.astype(jnp.bfloat16)
    d_up = d_up.astype(jnp.bfloat16)
    gate_local = jnp.einsum("rd,rf->df", rows_two, d_gate, preferred_element_type=jnp.float32)
    up_local = jnp.einsum("rd,rf->df", rows_two, d_up, preferred_element_type=jnp.float32)
    d_normed_two = jnp.einsum("rf,df->rd", d_gate, gate_back, preferred_element_type=jnp.float32)
    d_normed_two = d_normed_two + jnp.einsum(
        "rf,df->rd", d_up, up_back, preferred_element_type=jnp.float32
    )
    norm_two_pull = jax.vjp(rms_norm, hidden, gain_two)[1]
    d_hidden_norm, d_gain_two = norm_two_pull(
        scatter_rows(d_normed_two.reshape(seq_count, span, width))
    )
    d_hidden = out_grad.astype(jnp.float32) + d_hidden_norm
    branch_rows = gather_rows(d_hidden.astype(jnp.bfloat16)).reshape(row_count, width)
    out_local = jnp.einsum("rd,rp->dp", branch_rows, mixed, preferred_element_type=jnp.float32)
    d_mixed = jnp.dot(branch_rows, out_back, preferred_element_type=jnp.float32).astype(
        jnp.bfloat16
    )
    d_mixed = d_mixed.reshape(seq_count, span, local_heads, HEAD)
    d_query_parts = []
    d_key_parts = []
    d_value_parts = []
    d_bias = jnp.zeros((2, local_heads), jnp.float32)
    for seq in range(seq_count):
        key_rows = keys_all[seq].reshape(seq_length, local_heads, HEAD)
        value_rows = values_all[seq].reshape(seq_length, local_heads, HEAD)

        def back_block(carry, item, seq=seq, key_rows=key_rows, value_rows=value_rows):
            d_keys, d_values, bias_sum = carry
            first, lse_block = item
            query_block = queries[seq]
            query_var = my_variates[seq]
            query_seg = my_segments[seq]
            scores, same = scores_of(
                query_block, key_rows, query_var, variate_ids[seq], query_seg, segment_ids[seq]
            )
            probs = jnp.exp(scores - lse_block[:, :, None])
            probs_low = probs.astype(jnp.bfloat16)
            d_out = d_mixed[seq]
            d_probs = jnp.einsum(
                "qhd,khd->hqk", d_out, value_rows, preferred_element_type=jnp.float32
            )
            delta = jnp.sum(probs * d_probs, axis=-1, keepdims=True)
            d_scores = (probs * (d_probs - delta)).astype(jnp.bfloat16)
            d_query = (
                jnp.einsum("hqk,khd->qhd", d_scores, key_rows, preferred_element_type=jnp.float32)
                * scale
            )
            d_keys = (
                d_keys
                + jnp.einsum(
                    "hqk,qhd->khd", d_scores, query_block, preferred_element_type=jnp.float32
                )
                * scale
            )
            d_values = d_values + jnp.einsum(
                "hqk,qhd->khd", probs_low, d_out, preferred_element_type=jnp.float32
            )
            wide_scores = d_scores.astype(jnp.float32)
            same_sum = jnp.sum(jnp.where(same, wide_scores, 0.0), axis=(1, 2))
            diff_sum = jnp.sum(jnp.where(same, 0.0, wide_scores), axis=(1, 2))
            return ((d_keys, d_values, bias_sum + jnp.stack([same_sum, diff_sum])), d_query)

        zero_rows = jnp.zeros((seq_length, local_heads, HEAD), jnp.float32)
        (d_keys, d_values, bias_sum), d_query_blocks = lax.scan(
            back_block,
            (zero_rows, zero_rows, jnp.zeros((2, local_heads), jnp.float32)),
            (block_starts, lse_parts[seq]),
        )
        d_query_parts.append(d_query_blocks.reshape(span, local_heads, HEAD))
        d_key_parts.append(d_keys.reshape(seq_length, proj_width))
        d_value_parts.append(d_values.reshape(seq_length, proj_width))
        d_bias = d_bias + bias_sum
    d_keys_mine, d_values_mine = (
        lax.psum_scatter(
            jnp.stack(d_key_parts).astype(jnp.bfloat16), "ctx", scatter_dimension=1, tiled=True
        ).astype(jnp.float32),
        lax.psum_scatter(
            jnp.stack(d_value_parts).astype(jnp.bfloat16), "ctx", scatter_dimension=1, tiled=True
        ).astype(jnp.float32),
    )

    def rope_local(values):
        return rotate(values, my_times)

    rope_pull = jax.vjp(rope_local, queries_raw)[1]
    d_query_raw = (
        rope_pull(jnp.stack(d_query_parts))[0].astype(jnp.bfloat16).reshape(row_count, proj_width)
    )
    d_key_raw = (
        rope_pull(d_keys_mine.reshape(seq_count, span, local_heads, HEAD))[0]
        .astype(jnp.bfloat16)
        .reshape(row_count, proj_width)
    )
    d_value_low = d_values_mine.astype(jnp.bfloat16).reshape(row_count, proj_width)
    query_local = jnp.einsum("rd,rp->dp", rows_one, d_query_raw, preferred_element_type=jnp.float32)
    key_local = jnp.einsum("rd,rp->dp", rows_one, d_key_raw, preferred_element_type=jnp.float32)
    value_local = jnp.einsum("rd,rp->dp", rows_one, d_value_low, preferred_element_type=jnp.float32)
    d_normed_one = jnp.einsum(
        "rp,dp->rd", d_query_raw, query_back, preferred_element_type=jnp.float32
    )
    d_normed_one = d_normed_one + jnp.einsum(
        "rp,dp->rd", d_key_raw, key_back, preferred_element_type=jnp.float32
    )
    d_normed_one = d_normed_one + jnp.einsum(
        "rp,dp->rd", d_value_low, value_back, preferred_element_type=jnp.float32
    )
    norm_one_pull = jax.vjp(rms_norm, inputs, gain_one)[1]
    d_input_norm, d_gain_one = norm_one_pull(
        scatter_rows(d_normed_one.reshape(seq_count, span, width))
    )
    in_grad = (d_hidden + d_input_norm).astype(jnp.bfloat16)
    query_grad, key_grad, value_grad, out_weight_grad = (
        lax.psum_scatter(
            query_local.astype(jnp.bfloat16), ("fsdp", "ctx"), scatter_dimension=0, tiled=True
        ).astype(jnp.float32),
        lax.psum_scatter(
            key_local.astype(jnp.bfloat16), ("fsdp", "ctx"), scatter_dimension=0, tiled=True
        ).astype(jnp.float32),
        lax.psum_scatter(
            value_local.astype(jnp.bfloat16), ("fsdp", "ctx"), scatter_dimension=0, tiled=True
        ).astype(jnp.float32),
        lax.psum_scatter(
            out_local.astype(jnp.bfloat16), ("fsdp", "ctx"), scatter_dimension=0, tiled=True
        ).astype(jnp.float32),
    )
    gate_grad, up_grad, down_grad = (
        lax.psum_scatter(
            gate_local.astype(jnp.bfloat16), ("fsdp", "ctx"), scatter_dimension=0, tiled=True
        ).astype(jnp.float32),
        lax.psum_scatter(
            up_local.astype(jnp.bfloat16), ("fsdp", "ctx"), scatter_dimension=0, tiled=True
        ).astype(jnp.float32),
        lax.psum_scatter(
            down_local.astype(jnp.bfloat16), ("fsdp", "ctx"), scatter_dimension=0, tiled=True
        ).astype(jnp.float32),
    )
    head_offset = lax.axis_index("tp") * local_heads
    bias_full = lax.dynamic_update_slice_in_dim(
        jnp.zeros((2, HEADS), jnp.float32), d_bias, head_offset, 1
    )
    attn_gain_grad, ffn_gain_grad, bias_total = lax.psum(
        (d_gain_one, d_gain_two, bias_full), ("fsdp", "ctx", "tp")
    )
    bias_grad = lax.dynamic_slice_in_dim(bias_total, head_offset, local_heads, 1)
    return (
        layer_out,
        in_grad,
        attn_gain_grad,
        ffn_gain_grad,
        query_grad,
        key_grad,
        value_grad,
        out_weight_grad,
        bias_grad,
        gate_grad,
        up_grad,
        down_grad,
    )


def solution(mesh):
    in_specs = (
        P("fsdp", ("ctx", "tp"), None),
        P(),
        P(),
        P(("fsdp", "ctx"), "tp"),
        P(("fsdp", "ctx"), "tp"),
        P(("fsdp", "ctx"), "tp"),
        P(("fsdp", "ctx"), "tp"),
        P(None, "tp"),
        P(("fsdp", "ctx"), "tp"),
        P(("fsdp", "ctx"), "tp"),
        P(("fsdp", "ctx"), "tp"),
        P("fsdp", None),
        P("fsdp", None),
        P("fsdp", None),
        P("fsdp", ("ctx", "tp"), None),
    )
    out_specs = (
        P("fsdp", ("ctx", "tp"), None),
        P("fsdp", ("ctx", "tp"), None),
        P(),
        P(),
        P(("fsdp", "ctx"), "tp"),
        P(("fsdp", "ctx"), "tp"),
        P(("fsdp", "ctx"), "tp"),
        P(("fsdp", "ctx"), "tp"),
        P(None, "tp"),
        P(("fsdp", "ctx"), "tp"),
        P(("fsdp", "ctx"), "tp"),
        P(("fsdp", "ctx"), "tp"),
    )
    return jax.shard_map(shards, mesh=mesh, in_specs=in_specs, out_specs=out_specs, check_vma=False)
```

profile of v0, /device:TPU:0, one launch (start us, length us, event | category | flops | bytes accessed | tf_op | source)
XLA Modules:
  0.0 1151.3 jit_solution(9747962312075755871)
XLA Ops:
  15.6 33.3 %all_gather.49 = bf16[1024,256]{1,0:T(8,128)(2,1)S(1)} all-gather(bf16[128,256]{1,0:T(8,128)(2,1)} %param.18), channel_id=1, replica_groups=mesh['fsdp'=4,'ctx'=2,'tp'=4] {'fsdp','ctx'}, dimensions={0}, use_global_device_ids=true | all-gather | bytes 589824 | tf_op jit(solution)/shard_map/all_gather | solution.py:81
  48.9 31.6 %all_gather.50 = bf16[1024,256]{1,0:T(8,128)(2,1)S(1)} all-gather(bf16[128,256]{1,0:T(8,128)(2,1)} %param.19), channel_id=1, replica_groups=mesh['fsdp'=4,'ctx'=2,'tp'=4] {'fsdp','ctx'}, dimensions={0}, use_global_device_ids=true | all-gather | bytes 589824 | tf_op jit(solution)/shard_map/all_gather | solution.py:82
  80.5 31.9 %all_gather.47 = bf16[1024,256]{1,0:T(8,128)(2,1)S(1)} all-gather(bf16[128,256]{1,0:T(8,128)(2,1)} %param.20), channel_id=1, replica_groups=mesh['fsdp'=4,'ctx'=2,'tp'=4] {'fsdp','ctx'}, dimensions={0}, use_global_device_ids=true | all-gather | bytes 589824 | tf_op jit(solution)/shard_map/all_gather | solution.py:83
  112.3 31.6 %all_gather.52 = bf16[1024,256]{1,0:T(8,128)(2,1)S(1)} all-gather(bf16[128,256]{1,0:T(8,128)(2,1)} %param.21), channel_id=1, replica_groups=mesh['fsdp'=4,'ctx'=2,'tp'=4] {'fsdp','ctx'}, dimensions={0}, use_global_device_ids=true | all-gather | bytes 589824 | tf_op jit(solution)/shard_map/all_gather | solution.py:84
  144.9 3.3 convolution_convert_fusion.5
  156.3 14.2 %all-gather.12.cloned.1.call-done = bf16[2,1024,256]{2,1,0:T(8,128)(2,1)} async-done(((bf16[2,512,256]{2,1,0:T(8,128)(2,1)}), bf16[2,1024,256]{2,1,0:T(8,128)(2,1)}) %all-gather.12.cloned.1.call-update) | async-done | bytes 1048592 | tf_op jit(solution)/shard_map/all_gather | solution.py:101
  176.9 17.1 %all-gather.14.cloned.1.call-done = bf16[2,1024,256]{1,2,0:T(8,128)(2,1)} async-done(((bf16[2,512,256]{1,2,0:T(8,128)(2,1)}), bf16[2,1024,256]{1,2,0:T(8,128)(2,1)}) %all-gather.14.cloned.1.call-update) | async-done | bytes 1048592 | tf_op jit(solution)/shard_map/all_gather | solution.py:100
  196.1 4.1 fusion.69
  203.5 2.8 fusion.38
  207.4 4.2 fusion.70
  221.1 43.6 %reduce-scatter.16.cloned.1.call-done = f32[2,128,1024]{2,1,0:T(8,128)} async-done(((f32[2,512,1024]{2,1,0:T(8,128)}), f32[2,128,1024]{2,1,0:T(8,128)}) %reduce-scatter.16.cloned.1.call-update) | async-done | bytes 1048592 | tf_op jit(solution)/shard_map/reduce_scatter | solution.py:39
  269.3 2.9 all-gather.20.cloned.1.call-done
  272.2 23.0 %all-gather.16.cloned.1.call-done = bf16[2,512,1024]{2,1,0:T(8,128)(2,1)} async-done(((bf16[2,128,1024]{2,1,0:T(8,128)(2,1)}), bf16[2,512,1024]{2,1,0:T(8,128)(2,1)}) %all-gather.16.cloned.1.call-update) | async-done | bytes 2097168 | tf_op jit(solution)/shard_map/all_gather | solution.py:35
  295.3 6.6 fusion.72
  301.8 45.0 %all-gather.18.cloned.1.call-done = bf16[1024,1024]{1,0:T(8,128)(2,1)} async-done(((bf16[128,1024]{1,0:T(8,128)(2,1)}), bf16[1024,1024]{1,0:T(8,128)(2,1)}) %all-gather.18.cloned.1.call-update) | async-done | bytes 2097168 | tf_op jit(solution)/shard_map/all_gather | solution.py:148
  346.9 6.5 fusion.71
  353.4 16.1 %all-gather.24.cloned.1.call-done = bf16[2,512,1024]{2,1,0:T(8,128)(2,1)} async-done(((bf16[2,128,1024]{2,1,0:T(8,128)(2,1)}), bf16[2,512,1024]{2,1,0:T(8,128)(2,1)}) %all-gather.24.cloned.1.call-update) | async-done | bytes 2097168 | tf_op jit(solution)/shard_map/all_gather | solution.py:35
  369.5 51.7 %all-gather.22.cloned.1.call-done = bf16[1024,1024]{1,0:T(8,128)(2,1)} async-done(((bf16[128,1024]{1,0:T(8,128)(2,1)}), bf16[1024,1024]{1,0:T(8,128)(2,1)}) %all-gather.22.cloned.1.call-update) | async-done | bytes 2097168 | tf_op jit(solution)/shard_map/all_gather | solution.py:150
  421.2 9.9 multiply_convert_fusion.2
  434.2 4.4 convolution_add_fusion
  438.7 43.1 %reduce-scatter.20.cloned.1.call-done = f32[2,128,1024]{2,1,0:T(8,128)} async-done(((f32[2,512,1024]{2,1,0:T(8,128)}), f32[2,128,1024]{2,1,0:T(8,128)}) %reduce-scatter.20.cloned.1.call-update) | async-done | bytes 1048592 | tf_op jit(solution)/shard_map/reduce_scatter | solution.py:39
  486.5 22.2 %all-gather.26.cloned.1.call-done = bf16[2,512,1024]{2,1,0:T(8,128)(2,1)} async-done(((bf16[2,128,1024]{2,1,0:T(8,128)(2,1)}), bf16[2,512,1024]{2,1,0:T(8,128)(2,1)}) %all-gather.26.cloned.1.call-update) | async-done | bytes 2097168 | tf_op jit(solution)/shard_map/all_gather | solution.py:35
  511.2 5.8 fusion.24
  517.1 7.2 multiply_reduce_fusion.1
  533.1 8.7 fusion
  545.9 4.8 fusion.2
  554.9 6.0 convert_bitcast_fusion
  560.8 4.1 copy.67
  565.0 5.9 convolution_convert_fusion
  571.0 5.9 convolution_convert_fusion.1
  577.0 3.1 fusion.33
  580.2 4.5 fusion.36
  584.8 3.2 fusion.32
  588.3 4.5 fusion.37
  594.1 2.8 multiply_add_fusion.1
  602.8 3.2 convolution_convert_fusion.3
  611.5 6.7 fusion.73
  618.3 29.3 %reduce-scatter.40.cloned.1.call-done = bf16[128,1024]{1,0:T(8,128)(2,1)} async-done(((bf16[1024,1024]{1,0:T(8,128)(2,1)}), bf16[128,1024]{1,0:T(8,128)(2,1)}) %reduce-scatter.40.cloned.1.call-update) | async-done | bytes 262160
  649.6 68.4 %reduce-scatter.38.cloned.1.call-done = bf16[128,1024]{1,0:T(8,128)(2,1)} async-done(((bf16[1024,1024]{1,0:T(8,128)(2,1)}), bf16[128,1024]{1,0:T(8,128)(2,1)}) %reduce-scatter.38.cloned.1.call-update) | async-done | bytes 262160 | tf_op jit(solution)/shard_map/reduce_scatter | solution.py:305
  719.8 68.3 %reduce-scatter.36.cloned.1.call-done = bf16[128,1024]{1,0:T(8,128)(2,1)} async-done(((bf16[1024,1024]{1,0:T(8,128)(2,1)}), bf16[128,1024]{1,0:T(8,128)(2,1)}) %reduce-scatter.36.cloned.1.call-update) | async-done | bytes 262160 | tf_op jit(solution)/shard_map/reduce_scatter | solution.py:302
  790.1 62.4 %reduce-scatter.34.cloned.1.call-done = bf16[128,256]{1,0:T(8,128)(2,1)} async-done(((bf16[1024,256]{1,0:T(8,128)(2,1)}), bf16[128,256]{1,0:T(8,128)(2,1)}) %reduce-scatter.34.cloned.1.call-update) | async-done | bytes 65552 | tf_op jit(solution)/shard_map/reduce_scatter | solution.py:297
  854.0 63.0 %reduce-scatter.32.cloned.1.call-done = bf16[128,256]{1,0:T(8,128)(2,1)} async-done(((bf16[1024,256]{1,0:T(8,128)(2,1)}), bf16[128,256]{1,0:T(8,128)(2,1)}) %reduce-scatter.32.cloned.1.call-update) | async-done | bytes 65552 | tf_op jit(solution)/shard_map/reduce_scatter | solution.py:294
  918.5 63.3 %reduce-scatter.30.cloned.1.call-done = bf16[128,256]{1,0:T(8,128)(2,1)} async-done(((bf16[1024,256]{1,0:T(8,128)(2,1)}), bf16[128,256]{1,0:T(8,128)(2,1)}) %reduce-scatter.30.cloned.1.call-update) | async-done | bytes 65552 | tf_op jit(solution)/shard_map/reduce_scatter | solution.py:291
  983.4 63.6 %reduce-scatter.28.cloned.1.call-done = bf16[128,256]{1,0:T(8,128)(2,1)} async-done(((bf16[1024,256]{1,0:T(8,128)(2,1)}), bf16[128,256]{1,0:T(8,128)(2,1)}) %reduce-scatter.28.cloned.1.call-update) | async-done | bytes 65552 | tf_op jit(solution)/shard_map/reduce_scatter | solution.py:288
  1048.4 44.4 %reduce-scatter.26.cloned.1.call-done = f32[2,128,1024]{2,1,0:T(8,128)} async-done(((f32[2,512,1024]{2,1,0:T(8,128)}), f32[2,128,1024]{2,1,0:T(8,128)}) %reduce-scatter.26.cloned.1.call-update) | async-done | bytes 1048592 | tf_op jit(solution)/shard_map/reduce_scatter | solution.py:39
  1094.4 39.8 %all-reduce.4 = (f32[1024]{0:T(1024)}, f32[1024]{0:T(1024)}, f32[2,16]{1,0:T(2,128)S(1)}) all-reduce(f32[1024]{0:T(1024)S(1)} %get-tuple-element.206, f32[1024]{0:T(1024)S(1)} %copy-done.44, f32[2,16]{1,0:T(2,128)S(1)} %dynamic_update_slice.18), channel_id=1, replica_groups=mesh['fsdp'=4,'ctx'=2,'tp'=4] {'fsdp','ctx','tp'}, use_global_device_ids=true, to_apply=%region_17.18 | all-reduce | flops 2080 | bytes 16640 | tf_op jit(solution)/shard_map/psum | solution.py:316
  1134.9 5.8 reduce-scatter.18.cloned.1.call-done
  1140.7 3.0 fusion.44
  (259 shorter events, 97.3 us)
Async XLA Ops:
  8.0 136.9 %all-gather.10.cloned.1.call-start = ((), (), s32[]{:S(2)}) async-start(), calls=%async_computation.13 | async-start | bytes 2621440 | tf_op jit(solution)/shard_map/all_gather | solution.py:35
  13.2 157.4 %all-gather.12.cloned.1.call-start = ((), (), s32[]{:S(2)}) async-start(), calls=%async_computation.14 | async-start | bytes 1572864 | tf_op jit(solution)/shard_map/all_gather | solution.py:101
  80.5 67.8 %copy-start.43 = (s32[2,1024]{1,0:T(2,128)S(1)}, s32[2,1024]{1,0:T(2,128)}, u32[]{:S(2)}) copy-start(s32[2,1024]{1,0:T(2,128)} %param.26) | copy-start | bytes 24580
  112.3 36.2 %copy-start.23 = (bf16[1024,256]{1,0:T(8,128)(2,1)}, bf16[1024,256]{1,0:T(8,128)(2,1)S(1)}, u32[]{:S(2)}) copy-start(bf16[1024,256]{1,0:T(8,128)(2,1)S(1)} %all_gather.47) | copy-start | bytes 1572868
  144.0 73.3 %copy-start.13 = (bf16[1024,256]{1,0:T(8,128)(2,1)}, bf16[1024,256]{1,0:T(8,128)(2,1)S(1)}, u32[]{:S(2)}) copy-start(bf16[1024,256]{1,0:T(8,128)(2,1)S(1)} %all_gather.52) | copy-start | bytes 1572868
  144.9 51.2 %copy-start.11 = (pred[512,1024]{1,0:T(8,128)(4,1)}, pred[512,1024]{1,0:T(8,128)(4,1)S(1)}, u32[]{:S(2)}) copy-start(pred[512,1024]{1,0:T(8,128)(4,1)S(1)} %broadcast_compare_fusion) | copy-start | bytes 1572868
  148.2 45.8 %all-gather.14.cloned.1.call-start = ((), (), s32[]{:S(2)}) async-start(), calls=%async_computation.15 | async-start | bytes 1572864 | tf_op jit(solution)/shard_map/all_gather | solution.py:100
  152.4 55.0 %copy-start.7 = (bf16[2,512,4,32]{1,3,2,0:T(8,128)(2,1)}, bf16[2,512,4,32]{1,3,2,0:T(8,128)(2,1)S(1)}, u32[]{:S(2)}) copy-start(bf16[2,512,4,32]{1,3,2,0:T(8,128)(2,1)S(1)} %get-tuple-element.238) | copy-start | bytes 786436
  152.4 55.0 %copy-start.9 = (bf16[2,512,4,32]{1,3,2,0:T(8,128)(2,1)}, bf16[2,512,4,32]{1,3,2,0:T(8,128)(2,1)S(1)}, u32[]{:S(2)}) copy-start(bf16[2,512,4,32]{1,3,2,0:T(8,128)(2,1)S(1)} %get-tuple-element.239) | copy-start | bytes 786436
  153.4 111.4 %reduce-scatter.16.cloned.1.call-start = ((), (), s32[]{:S(2)}) async-start(), calls=%async_computation.16 | async-start | bytes 5242880 | tf_op jit(solution)/shard_map/reduce_scatter | solution.py:39
  153.6 46.5 %copy-start.55 = (f32[4]{0:T(128)}, f32[4]{0:T(128)S(1)}, u32[]{:S(2)}) copy-start(f32[4]{0:T(128)S(1)} %get-tuple-element.264) | copy-start | bytes 52
  153.6 46.5 %copy-start.56 = (f32[4]{0:T(128)}, f32[4]{0:T(128)S(1)}, u32[]{:S(2)}) copy-start(f32[4]{0:T(128)S(1)} %get-tuple-element.265) | copy-start | bytes 52
  154.0 53.4 %copy-start.14 = (pred[512,1024]{1,0:T(8,128)(4,1)}, pred[512,1024]{1,0:T(8,128)(4,1)S(1)}, u32[]{:S(2)}) copy-start(pred[512,1024]{1,0:T(8,128)(4,1)S(1)} %broadcast_compare_fusion.2) | copy-start | bytes 1572868
  217.3 47.5 %copy-start.4 = (bf16[2,128,1024]{2,1,0:T(8,128)(2,1)S(1)}, bf16[2,128,1024]{2,1,0:T(8,128)(2,1)}, u32[]{:S(2)}) copy-start(bf16[2,128,1024]{2,1,0:T(8,128)(2,1)} %param.15) | copy-start | bytes 1572868
  220.0 52.2 %all-gather.20.cloned.1.call-start = ((), (), s32[]{:S(2)}) async-start(), calls=%async_computation.19 | async-start | bytes 2359296 | tf_op jit(solution)/shard_map/all_gather | solution.py:149
  220.6 74.7 %all-gather.16.cloned.1.call-start = ((), (), s32[]{:S(2)}) async-start(), calls=%async_computation.17 | async-start | bytes 2621440 | tf_op jit(solution)/shard_map/all_gather | solution.py:35
  221.1 262.7 %copy-start.31 = (f32[1024]{0:T(1024)}, f32[1024]{0:T(1024)S(1)}, u32[]{:S(2)}) copy-start(f32[1024]{0:T(1024)S(1)} %convert_element_type.167) | copy-start | bytes 12292
  266.2 217.6 %copy-start.41 = (f32[2,128]{1,0:T(2,128)}, f32[2,128]{1,0:T(2,128)S(1)}, u32[]{:S(2)}) copy-start(f32[2,128]{1,0:T(2,128)S(1)} %fusion.57) | copy-start | bytes 3076
  267.2 79.7 %all-gather.18.cloned.1.call-start = ((), (), s32[]{:S(2)}) async-start(), calls=%async_computation.18 | async-start | bytes 2359296 | tf_op jit(solution)/shard_map/all_gather | solution.py:148
  267.8 101.7 %all-gather.24.cloned.1.call-start = ((), (), s32[]{:S(2)}) async-start(), calls=%async_computation.22 | async-start | bytes 2621440 | tf_op jit(solution)/shard_map/all_gather | solution.py:35
  268.5 152.7 %all-gather.22.cloned.1.call-start = ((), (), s32[]{:S(2)}) async-start(), calls=%async_computation.20 | async-start | bytes 2359296 | tf_op jit(solution)/shard_map/all_gather | solution.py:150
  269.3 212.5 %reduce-scatter.20.cloned.1.call-start = ((), (), s32[]{:S(2)}) async-start(), calls=%async_computation.23 | async-start | bytes 5242880 | tf_op jit(solution)/shard_map/reduce_scatter | solution.py:39
  438.6 45.3 %copy-start.6 = (bf16[2,128,1024]{2,1,0:T(8,128)(2,1)S(1)}, bf16[2,128,1024]{2,1,0:T(8,128)(2,1)}, u32[]{:S(2)}) copy-start(bf16[2,128,1024]{2,1,0:T(8,128)(2,1)} %param.29) | copy-start | bytes 1572868
  438.6 47.9 %copy-start.36 = (f32[4,512]{1,0:T(4,128)S(1)}, f32[4,512]{1,0:T(4,128)}, u32[]{:S(2)}) copy-start(f32[4,512]{1,0:T(4,128)} %copy-done.35) | copy-start | bytes 24580
  438.6 47.9 %copy-start.38 = (f32[4,512]{1,0:T(4,128)S(1)}, f32[4,512]{1,0:T(4,128)}, u32[]{:S(2)}) copy-start(f32[4,512]{1,0:T(4,128)} %copy-done.37) | copy-start | bytes 24580
  438.6 47.9 %copy-start.40 = (f32[4,512]{1,0:T(4,128)S(1)}, f32[4,512]{1,0:T(4,128)}, u32[]{:S(2)}) copy-start(f32[4,512]{1,0:T(4,128)} %copy-done.39) | copy-start | bytes 24580
  438.6 70.1 %all-gather.26.cloned.1.call-start = ((), (), s32[]{:S(2)}) async-start(), calls=%async_computation.24 | async-start | bytes 2621440 | tf_op jit(solution)/shard_map/all_gather | solution.py:35
  486.2 98.6 %reduce-scatter.24.cloned.1.call-start = ((), (), s32[]{:S(2)}) async-start(), calls=%async_computation.26 | async-start | bytes 1572864 | tf_op jit(solution)/shard_map/reduce_scatter | solution.py:252
  533.0 59.9 %reduce-scatter.22.cloned.1.call-start = ((), (), s32[]{:S(2)}) async-start(), calls=%async_computation.25 | async-start | bytes 1572864 | tf_op jit(solution)/shard_map/reduce_scatter | solution.py:249
  554.6 93.0 %reduce-scatter.40.cloned.1.call-start = ((), (), s32[]{:S(2)}) async-start(), calls=%async_computation.34 | async-start | bytes 2359296
  564.9 153.1 %reduce-scatter.38.cloned.1.call-start = ((), (), s32[]{:S(2)}) async-start(), calls=%async_computation.33 | async-start | bytes 2359296 | tf_op jit(solution)/shard_map/reduce_scatter | solution.py:305
  570.9 217.2 %reduce-scatter.36.cloned.1.call-start = ((), (), s32[]{:S(2)}) async-start(), calls=%async_computation.32 | async-start | bytes 2359296 | tf_op jit(solution)/shard_map/reduce_scatter | solution.py:302
  576.9 275.5 %reduce-scatter.34.cloned.1.call-start = ((), (), s32[]{:S(2)}) async-start(), calls=%async_computation.31 | async-start | bytes 589824 | tf_op jit(solution)/shard_map/reduce_scatter | solution.py:297
  580.2 336.8 %reduce-scatter.32.cloned.1.call-start = ((), (), s32[]{:S(2)}) async-start(), calls=%async_computation.30 | async-start | bytes 589824 | tf_op jit(solution)/shard_map/reduce_scatter | solution.py:294
  588.0 393.8 %reduce-scatter.30.cloned.1.call-start = ((), (), s32[]{:S(2)}) async-start(), calls=%async_computation.29 | async-start | bytes 589824 | tf_op jit(solution)/shard_map/reduce_scatter | solution.py:291
  600.0 447.0 %reduce-scatter.28.cloned.1.call-start = ((), (), s32[]{:S(2)}) async-start(), calls=%async_computation.28 | async-start | bytes 589824 | tf_op jit(solution)/shard_map/reduce_scatter | solution.py:288
  605.9 486.9 %reduce-scatter.26.cloned.1.call-start = ((), (), s32[]{:S(2)}) async-start(), calls=%async_computation.27 | async-start | bytes 5242880 | tf_op jit(solution)/shard_map/reduce_scatter | solution.py:39
  611.5 529.1 %reduce-scatter.18.cloned.1.call-start = ((), (), s32[]{:S(2)}) async-start(), calls=%async_computation.21 | async-start | bytes 5242880 | tf_op jit(solution)/shard_map/reduce_scatter | solution.py:39
  618.2 171.7 %copy-start.51 = (f32[4]{0:T(128)S(1)}, f32[4]{0:T(128)}, u32[]{:S(2)}) copy-start(f32[4]{0:T(128)} %get-tuple-element.202) | copy-start | bytes 52
  618.2 171.7 %copy-start.52 = (f32[4]{0:T(128)S(1)}, f32[4]{0:T(128)}, u32[]{:S(2)}) copy-start(f32[4]{0:T(128)} %get-tuple-element.203) | copy-start | bytes 52
  618.2 474.6 %copy-start.34 = (f32[1024]{0:T(1024)S(1)}, f32[1024]{0:T(1024)}, u32[]{:S(2)}) copy-start(f32[1024]{0:T(1024)} %copy-done.33) | copy-start | bytes 12292
  618.2 474.6 %copy-start.46 = (f32[2,128]{1,0:T(2,128)S(1)}, f32[2,128]{1,0:T(2,128)}, u32[]{:S(2)}) copy-start(f32[2,128]{1,0:T(2,128)} %copy-done.45) | copy-start | bytes 3076
  618.2 476.2 %copy-start.44 = (f32[1024]{0:T(1024)S(1)}, f32[1024]{0:T(1024)}, u32[]{:S(2)}) copy-start(f32[1024]{0:T(1024)} %get-tuple-element.204) | copy-start | bytes 12292
  618.2 516.6 %copy-start.48 = (f32[2,128]{1,0:T(2,128)S(1)}, f32[2,128]{1,0:T(2,128)}, u32[]{:S(2)}) copy-start(f32[2,128]{1,0:T(2,128)} %copy-done.47) | copy-start | bytes 3076
  618.2 522.4 %copy-start.5 = (f32[2,128,1024]{2,1,0:T(8,128)S(1)}, f32[2,128,1024]{2,1,0:T(8,128)}, u32[]{:S(2)}) copy-start(f32[2,128,1024]{2,1,0:T(8,128)} %reduce-scatter.20.cloned.1.call-done) | copy-start | bytes 3145732
  618.3 522.4 %copy-start.32 = (f32[1024]{0:T(1024)S(1)}, f32[1024]{0:T(1024)}, u32[]{:S(2)}) copy-start(f32[1024]{0:T(1024)} %copy-done.31) | copy-start | bytes 12292
  618.3 522.4 %copy-start.42 = (f32[2,128]{1,0:T(2,128)S(1)}, f32[2,128]{1,0:T(2,128)}, u32[]{:S(2)}) copy-start(f32[2,128]{1,0:T(2,128)} %copy-done.41) | copy-start | bytes 3076
  618.3 522.4 %copy-start.50 = (f32[2,128]{1,0:T(2,128)S(1)}, f32[2,128]{1,0:T(2,128)}, u32[]{:S(2)}) copy-start(f32[2,128]{1,0:T(2,128)} %copy-done.49) | copy-start | bytes 3076
  (41 other events, 200.3 us)
Sparse Core Ops, SparseCore 0:
  13.3 25.2 all-gather.9
  148.3 22.1 all-gather.11
  172.7 21.2 all-gather.13
  220.1 44.5 reduce-scatter.15
  438.7 42.9 reduce-scatter.19
  533.1 20.3 reduce-scatter.23
  555.8 20.3 reduce-scatter.21
  579.7 67.8 reduce-scatter.39
  651.1 66.8 reduce-scatter.37
  721.4 66.6 reduce-scatter.35
  791.5 60.9 reduce-scatter.33
  856.0 60.9 reduce-scatter.31
  920.9 60.8 reduce-scatter.29
  986.0 60.9 reduce-scatter.27
  1049.3 43.4 reduce-scatter.25
  1095.4 45.2 reduce-scatter.17
Sparse Core Ops, SparseCore 1:
  222.9 49.3 all-gather.19
  274.3 20.9 all-gather.15
  297.5 49.3 all-gather.17
  348.5 20.9 all-gather.23
  371.8 49.3 all-gather.21
  486.3 22.4 all-gather.25
where the time goes:
time: 1160 us; the launch traced here: 1150 us
  waiting for transfers between devices  750 us (65%)
  blocking collectives  168 us (14%)
  matrix products  124 us (11%)
  other arithmetic  56.5 us (5%)
  local copies, waits for them, and re-layouts  33 us (3%)
  between operations  16.9 us (1%)
    reduce_scatter x4, waiting for transfers between devices, scatter_rows(): return lax.psum_scatter(values, 'tp', scatter_dimension=1, tiled=True)  137 us
    reduce_scatter x1, waiting for transfers between devices, shards(): lax.psum_scatter(up_local.astype(jnp.bfloat16), ('fsdp', 'ctx'), scatter_...  68.4 us
    reduce_scatter x1, waiting for transfers between devices, shards(): lax.psum_scatter(gate_local.astype(jnp.bfloat16), ('fsdp', 'ctx'), scatte...  68.3 us
    reduce_scatter x1, waiting for transfers between devices, shards(): lax.psum_scatter(query_local.astype(jnp.bfloat16), ('fsdp', 'ctx'), scatt...  63.6 us
    reduce_scatter x1, waiting for transfers between devices, shards(): lax.psum_scatter(key_local.astype(jnp.bfloat16), ('fsdp', 'ctx'), scatter...  63.3 us
    reduce_scatter x1, waiting for transfers between devices, shards(): lax.psum_scatter(value_local.astype(jnp.bfloat16), ('fsdp', 'ctx'), scatt...  63 us
    reduce_scatter x1, waiting for transfers between devices, shards(): lax.psum_scatter(out_local.astype(jnp.bfloat16), ('fsdp', 'ctx'), scatter...  62.4 us
    all_gather x4, waiting for transfers between devices, gather_rows(): return lax.all_gather(values, 'tp', axis=1, tiled=True)  61.4 us
  transfers between devices with their start and end apart: 22, of which 19 were waited for; matrix products, arithmetic and copies ran while one was open for 11% of the time, Pallas kernels for 0%

commit v1 on v0

--- a/solution.py
+++ b/solution.py
@@ -7,6 +7,24 @@
 HEAD = 64
 EPS = 1e-05
 NEG = -1e30
+
+
+def ring_gather(value, axis, dim):
+    ways, here, lap = (lax.axis_size(axis), lax.axis_index(axis), value.shape[dim])
+    shape = [n * ways if d == dim else n for d, n in enumerate(value.shape)]
+    full = lax.dynamic_update_slice_in_dim(
+        jnp.zeros(shape, value.dtype), value, here * lap, axis=dim
+    )
+    going_up = going_down = value
+    for far in range(1, ways // 2 + 1):
+        going_up = lax.ppermute(going_up, axis, [(d, (d + 1) % ways) for d in range(ways)])
+        full = lax.dynamic_update_slice_in_dim(full, going_up, (here - far) % ways * lap, axis=dim)
+        if 2 * far < ways:
+            going_down = lax.ppermute(going_down, axis, [(d, (d - 1) % ways) for d in range(ways)])
+            full = lax.dynamic_update_slice_in_dim(
+                full, going_down, (here + far) % ways * lap, axis=dim
+            )
+    return full
 
 
 def rms_norm(values, gain):
@@ -80,7 +98,7 @@
     query_full, key_full, value_full, out_full = (
         lax.all_gather(query_weight, ("fsdp", "ctx"), axis=0, tiled=True),
         lax.all_gather(key_weight, ("fsdp", "ctx"), axis=0, tiled=True),
-        lax.all_gather(value_weight, ("fsdp", "ctx"), axis=0, tiled=True),
+        ring_gather(value_weight, ("fsdp", "ctx"), 0),
         lax.all_gather(out_weight, ("fsdp", "ctx"), axis=0, tiled=True),
     )
     queries_raw = jnp.dot(rows_one, query_full, preferred_element_type=jnp.float32).reshape(

time: 1160 us -> 1150 us (level)
  waiting for transfers between devices: 750 us -> 726 us
  starting transfers between devices: 2.17 us -> 17.8 us
    unnamed x23, waiting for transfers between devices: 32 us -> 2.73 us
    ppermute x0 -> x7, starting transfers between devices: none -> 15.6 us  [the longest x3 12.5 us: ring_gather(): lax.ppermute(going_down, axis, [(d, (d - 1) % ways) for d in range(ways)])]
  transfers between devices with their start and end apart: 22 -> 29, of which waited for: 19 -> 21; matrix products, arithmetic and copies ran while one was open for 11% -> 11% of each run, Pallas kernels for 0% -> 0%
where the time goes in v1:
time: 1150 us; the launch traced here: 1140 us
  waiting for transfers between devices  726 us (63%)
  blocking collectives  169 us (15%)
  matrix products  123 us (11%)
  other arithmetic  56.4 us (5%)
  local copies, waits for them, and re-layouts  33.4 us (3%)
  starting transfers between devices  17.8 us (2%)
  between operations  17 us (1%)
    reduce_scatter x4, waiting for transfers between devices, scatter_rows(): return lax.psum_scatter(values, 'tp', scatter_dimension=1, tiled=True)  137 us
    reduce_scatter x1, waiting for transfers between devices, shards(): lax.psum_scatter(gate_local.astype(jnp.bfloat16), ('fsdp', 'ctx'), scatte...  68.3 us
    reduce_scatter x1, waiting for transfers between devices, shards(): lax.psum_scatter(up_local.astype(jnp.bfloat16), ('fsdp', 'ctx'), scatter_...  65.8 us
    reduce_scatter x1, waiting for transfers between devices, shards(): lax.psum_scatter(query_local.astype(jnp.bfloat16), ('fsdp', 'ctx'), scatt...  63.7 us
    reduce_scatter x1, waiting for transfers between devices, shards(): lax.psum_scatter(key_local.astype(jnp.bfloat16), ('fsdp', 'ctx'), scatter...  63.3 us
    reduce_scatter x1, waiting for transfers between devices, shards(): lax.psum_scatter(value_local.astype(jnp.bfloat16), ('fsdp', 'ctx'), scatt...  63 us
    reduce_scatter x1, waiting for transfers between devices, shards(): lax.psum_scatter(out_local.astype(jnp.bfloat16), ('fsdp', 'ctx'), scatter...  62.3 us
    all_gather x4, waiting for transfers between devices, gather_rows(): return lax.all_gather(values, 'tp', axis=1, tiled=True)  61.4 us
  transfers between devices with their start and end apart: 29, of which 21 were waited for; matrix products, arithmetic and copies ran while one was open for 11% of the time, Pallas kernels for 0%

profile of v1, /device:TPU:0, one launch (start us, length us, event | category | flops | bytes accessed | tf_op | source)
XLA Modules:
  0.0 1142.2 jit_solution(18428725759862909233)
XLA Ops:
  13.2 3.0 collective-permute-start
  16.2 3.1 collective-permute-start.1
  21.7 31.9 %all_gather.47 = bf16[1024,256]{1,0:T(8,128)(2,1)S(1)} all-gather(bf16[128,256]{1,0:T(8,128)(2,1)} %param.18), channel_id=1, replica_groups=mesh['fsdp'=4,'ctx'=2,'tp'=4] {'fsdp','ctx'}, dimensions={0}, use_global_device_ids=true | all-gather | bytes 589824 | tf_op jit(solution)/shard_map/all_gather | solution.py:99
  53.6 31.7 %all_gather.48 = bf16[1024,256]{1,0:T(8,128)(2,1)S(1)} all-gather(bf16[128,256]{1,0:T(8,128)(2,1)} %param.19), channel_id=1, replica_groups=mesh['fsdp'=4,'ctx'=2,'tp'=4] {'fsdp','ctx'}, dimensions={0}, use_global_device_ids=true | all-gather | bytes 589824 | tf_op jit(solution)/shard_map/all_gather | solution.py:100
  85.3 31.8 %all_gather.50 = bf16[1024,256]{1,0:T(8,128)(2,1)S(1)} all-gather(bf16[128,256]{1,0:T(8,128)(2,1)} %param.21), channel_id=1, replica_groups=mesh['fsdp'=4,'ctx'=2,'tp'=4] {'fsdp','ctx'}, dimensions={0}, use_global_device_ids=true | all-gather | bytes 589824 | tf_op jit(solution)/shard_map/all_gather | solution.py:102
  118.2 4.7 collective-permute-start.3
  125.2 4.7 collective-permute-start.5
  132.2 6.9 collective-permute-done.6
  139.1 3.1 convolution_convert_fusion.5
  150.4 10.7 all-gather.12.cloned.1.call-done
  167.5 17.1 %all-gather.14.cloned.1.call-done = bf16[2,1024,256]{1,2,0:T(8,128)(2,1)} async-done(((bf16[2,512,256]{1,2,0:T(8,128)(2,1)}), bf16[2,1024,256]{1,2,0:T(8,128)(2,1)}) %all-gather.14.cloned.1.call-update) | async-done | bytes 1048592 | tf_op jit(solution)/shard_map/all_gather | solution.py:118
  186.7 4.1 fusion.69
  198.1 4.2 fusion.70
  211.8 43.6 %reduce-scatter.16.cloned.1.call-done = f32[2,128,1024]{2,1,0:T(8,128)} async-done(((f32[2,512,1024]{2,1,0:T(8,128)}), f32[2,128,1024]{2,1,0:T(8,128)}) %reduce-scatter.16.cloned.1.call-update) | async-done | bytes 1048592 | tf_op jit(solution)/shard_map/reduce_scatter | solution.py:57
  262.9 23.0 %all-gather.16.cloned.1.call-done = bf16[2,512,1024]{2,1,0:T(8,128)(2,1)} async-done(((bf16[2,128,1024]{2,1,0:T(8,128)(2,1)}), bf16[2,512,1024]{2,1,0:T(8,128)(2,1)}) %all-gather.16.cloned.1.call-update) | async-done | bytes 2097168 | tf_op jit(solution)/shard_map/all_gather | solution.py:53
  285.9 6.6 fusion.72
  292.5 45.0 %all-gather.18.cloned.1.call-done = bf16[1024,1024]{1,0:T(8,128)(2,1)} async-done(((bf16[128,1024]{1,0:T(8,128)(2,1)}), bf16[1024,1024]{1,0:T(8,128)(2,1)}) %all-gather.18.cloned.1.call-update) | async-done | bytes 2097168 | tf_op jit(solution)/shard_map/all_gather | solution.py:166
  337.5 6.6 fusion.71
  344.1 16.1 %all-gather.24.cloned.1.call-done = bf16[2,512,1024]{2,1,0:T(8,128)(2,1)} async-done(((bf16[2,128,1024]{2,1,0:T(8,128)(2,1)}), bf16[2,512,1024]{2,1,0:T(8,128)(2,1)}) %all-gather.24.cloned.1.call-update) | async-done | bytes 2097168 | tf_op jit(solution)/shard_map/all_gather | solution.py:53
  360.1 51.7 %all-gather.22.cloned.1.call-done = bf16[1024,1024]{1,0:T(8,128)(2,1)} async-done(((bf16[128,1024]{1,0:T(8,128)(2,1)}), bf16[1024,1024]{1,0:T(8,128)(2,1)}) %all-gather.22.cloned.1.call-update) | async-done | bytes 2097168 | tf_op jit(solution)/shard_map/all_gather | solution.py:168
  411.9 9.9 multiply_convert_fusion.2
  424.8 4.4 convolution_add_fusion
  429.3 43.1 %reduce-scatter.20.cloned.1.call-done = f32[2,128,1024]{2,1,0:T(8,128)} async-done(((f32[2,512,1024]{2,1,0:T(8,128)}), f32[2,128,1024]{2,1,0:T(8,128)}) %reduce-scatter.20.cloned.1.call-update) | async-done | bytes 1048592 | tf_op jit(solution)/shard_map/reduce_scatter | solution.py:57
  477.2 22.2 %all-gather.26.cloned.1.call-done = bf16[2,512,1024]{2,1,0:T(8,128)(2,1)} async-done(((bf16[2,128,1024]{2,1,0:T(8,128)(2,1)}), bf16[2,512,1024]{2,1,0:T(8,128)(2,1)}) %all-gather.26.cloned.1.call-update) | async-done | bytes 2097168 | tf_op jit(solution)/shard_map/all_gather | solution.py:53
  501.9 5.8 fusion.24
  507.7 7.3 multiply_reduce_fusion.1
  523.8 8.7 fusion
  536.6 4.8 fusion.2
  545.6 6.0 convert_bitcast_fusion
  551.5 4.1 copy.67
  555.7 5.9 convolution_convert_fusion
  561.7 5.9 convolution_convert_fusion.1
  567.8 3.2 fusion.33
  571.0 4.5 fusion.36
  575.6 3.2 fusion.32
  579.1 4.5 fusion.37
  590.9 33.5 %all_gather.57 = bf16[1024,256]{1,0:T(8,128)(2,1)} all-gather(bf16[128,256]{1,0:T(8,128)(2,1)S(1)} %copy-done.31), channel_id=1, replica_groups=mesh['fsdp'=4,'ctx'=2,'tp'=4] {'fsdp','ctx'}, dimensions={0}, use_global_device_ids=true | all-gather | bytes 589824 | tf_op jit(solution)/shard_map/all_gather | solution.py:180
  634.3 6.7 fusion.73
  643.2 65.8 %reduce-scatter.38.cloned.1.call-done = bf16[128,1024]{1,0:T(8,128)(2,1)} async-done(((bf16[1024,1024]{1,0:T(8,128)(2,1)}), bf16[128,1024]{1,0:T(8,128)(2,1)}) %reduce-scatter.38.cloned.1.call-update) | async-done | bytes 262160 | tf_op jit(solution)/shard_map/reduce_scatter | solution.py:323
  710.8 68.3 %reduce-scatter.36.cloned.1.call-done = bf16[128,1024]{1,0:T(8,128)(2,1)} async-done(((bf16[1024,1024]{1,0:T(8,128)(2,1)}), bf16[128,1024]{1,0:T(8,128)(2,1)}) %reduce-scatter.36.cloned.1.call-update) | async-done | bytes 262160 | tf_op jit(solution)/shard_map/reduce_scatter | solution.py:320
  781.1 62.3 %reduce-scatter.34.cloned.1.call-done = bf16[128,256]{1,0:T(8,128)(2,1)} async-done(((bf16[1024,256]{1,0:T(8,128)(2,1)}), bf16[128,256]{1,0:T(8,128)(2,1)}) %reduce-scatter.34.cloned.1.call-update) | async-done | bytes 65552 | tf_op jit(solution)/shard_map/reduce_scatter | solution.py:315
  844.9 63.0 %reduce-scatter.32.cloned.1.call-done = bf16[128,256]{1,0:T(8,128)(2,1)} async-done(((bf16[1024,256]{1,0:T(8,128)(2,1)}), bf16[128,256]{1,0:T(8,128)(2,1)}) %reduce-scatter.32.cloned.1.call-update) | async-done | bytes 65552 | tf_op jit(solution)/shard_map/reduce_scatter | solution.py:312
  909.4 63.3 %reduce-scatter.30.cloned.1.call-done = bf16[128,256]{1,0:T(8,128)(2,1)} async-done(((bf16[1024,256]{1,0:T(8,128)(2,1)}), bf16[128,256]{1,0:T(8,128)(2,1)}) %reduce-scatter.30.cloned.1.call-update) | async-done | bytes 65552 | tf_op jit(solution)/shard_map/reduce_scatter | solution.py:309
  974.2 63.7 %reduce-scatter.28.cloned.1.call-done = bf16[128,256]{1,0:T(8,128)(2,1)} async-done(((bf16[1024,256]{1,0:T(8,128)(2,1)}), bf16[128,256]{1,0:T(8,128)(2,1)}) %reduce-scatter.28.cloned.1.call-update) | async-done | bytes 65552 | tf_op jit(solution)/shard_map/reduce_scatter | solution.py:306
  1039.4 44.4 %reduce-scatter.26.cloned.1.call-done = f32[2,128,1024]{2,1,0:T(8,128)} async-done(((f32[2,512,1024]{2,1,0:T(8,128)}), f32[2,128,1024]{2,1,0:T(8,128)}) %reduce-scatter.26.cloned.1.call-update) | async-done | bytes 1048592 | tf_op jit(solution)/shard_map/reduce_scatter | solution.py:57
  1085.4 39.8 %all-reduce.4 = (f32[1024]{0:T(1024)}, f32[1024]{0:T(1024)}, f32[2,16]{1,0:T(2,128)S(1)}) all-reduce(f32[1024]{0:T(1024)S(1)} %get-tuple-element.206, f32[1024]{0:T(1024)S(1)} %copy-done.45, f32[2,16]{1,0:T(2,128)S(1)} %dynamic_update_slice.50), channel_id=1, replica_groups=mesh['fsdp'=4,'ctx'=2,'tp'=4] {'fsdp','ctx','tp'}, use_global_device_ids=true, to_apply=%region_17.18 | all-reduce | flops 2080 | bytes 16640 | tf_op jit(solution)/shard_map/psum | solution.py:334
  1125.8 5.8 reduce-scatter.18.cloned.1.call-done
  1131.6 3.0 fusion.44
  (286 shorter events, 112.3 us)
Async XLA Ops:
  8.0 110.1 %copy-start.30 = (bf16[128,256]{1,0:T(8,128)(2,1)S(1)}, bf16[128,256]{1,0:T(8,128)(2,1)}, u32[]{:S(2)}) copy-start(bf16[128,256]{1,0:T(8,128)(2,1)} %param.20) | copy-start | bytes 196612
  8.0 131.1 %all-gather.10.cloned.1.call-start = ((), (), s32[]{:S(2)}) async-start(), calls=%async_computation.13 | async-start | bytes 2621440 | tf_op jit(solution)/shard_map/all_gather | solution.py:53
  13.2 148.0 %all-gather.12.cloned.1.call-start = ((), (), s32[]{:S(2)}) async-start(), calls=%async_computation.14 | async-start | bytes 1572864 | tf_op jit(solution)/shard_map/all_gather | solution.py:119
  13.2 104.9 %collective-permute-start = (bf16[128,256]{1,0:T(8,128)(2,1)}, bf16[128,256]{1,0:T(8,128)(2,1)S(1)}, u32[]{:S(2)}, u32[]{:S(2)}) collective-permute-start(bf16[128,256]{1,0:T(8,128)(2,1)} %param.20), channel_id=1, source_target_pairs={{0,4},{4,8},{8,12},{12,16},{16,20},{20,24},{24,28},{28,0},{1,5},{5... | collective-permute-start | bytes 196616 | tf_op jit(solution)/shard_map/ppermute | solution.py:20
  16.2 102.0 %collective-permute-start.1 = (bf16[128,256]{1,0:T(8,128)(2,1)}, bf16[128,256]{1,0:T(8,128)(2,1)S(1)}, u32[]{:S(2)}, u32[]{:S(2)}) collective-permute-start(bf16[128,256]{1,0:T(8,128)(2,1)} %param.20), channel_id=1, source_target_pairs={{0,28},{4,0},{8,4},{12,8},{16,12},{20,16},{24,20},{28,24},{1,29},{... | collective-permute-start | bytes 196616 | tf_op jit(solution)/shard_map/ppermute | solution.py:23
  117.1 90.8 %copy-start.13 = (bf16[1024,256]{1,0:T(8,128)(2,1)}, bf16[1024,256]{1,0:T(8,128)(2,1)S(1)}, u32[]{:S(2)}) copy-start(bf16[1024,256]{1,0:T(8,128)(2,1)S(1)} %all_gather.50) | copy-start | bytes 1572868
  118.0 68.7 %copy-start.11 = (pred[512,1024]{1,0:T(8,128)(4,1)}, pred[512,1024]{1,0:T(8,128)(4,1)S(1)}, u32[]{:S(2)}) copy-start(pred[512,1024]{1,0:T(8,128)(4,1)S(1)} %broadcast_compare_fusion) | copy-start | bytes 1572868
  118.1 7.0 collective-permute-start.2
  118.2 6.9 collective-permute-start.3
  125.2 7.0 collective-permute-start.4
  125.2 7.0 collective-permute-start.5
  132.1 7.0 collective-permute-start.6
  142.2 42.4 %all-gather.14.cloned.1.call-start = ((), (), s32[]{:S(2)}) async-start(), calls=%async_computation.15 | async-start | bytes 1572864 | tf_op jit(solution)/shard_map/all_gather | solution.py:118
  146.4 51.6 %copy-start.7 = (bf16[2,512,4,32]{1,3,2,0:T(8,128)(2,1)}, bf16[2,512,4,32]{1,3,2,0:T(8,128)(2,1)S(1)}, u32[]{:S(2)}) copy-start(bf16[2,512,4,32]{1,3,2,0:T(8,128)(2,1)S(1)} %get-tuple-element.238) | copy-start | bytes 786436
  146.4 51.6 %copy-start.9 = (bf16[2,512,4,32]{1,3,2,0:T(8,128)(2,1)}, bf16[2,512,4,32]{1,3,2,0:T(8,128)(2,1)S(1)}, u32[]{:S(2)}) copy-start(bf16[2,512,4,32]{1,3,2,0:T(8,128)(2,1)S(1)} %get-tuple-element.239) | copy-start | bytes 786436
  147.4 108.0 %reduce-scatter.16.cloned.1.call-start = ((), (), s32[]{:S(2)}) async-start(), calls=%async_computation.16 | async-start | bytes 5242880 | tf_op jit(solution)/shard_map/reduce_scatter | solution.py:57
  148.1 50.0 %copy-start.14 = (pred[512,1024]{1,0:T(8,128)(4,1)}, pred[512,1024]{1,0:T(8,128)(4,1)S(1)}, u32[]{:S(2)}) copy-start(pred[512,1024]{1,0:T(8,128)(4,1)S(1)} %broadcast_compare_fusion.2) | copy-start | bytes 1572868
  210.7 52.2 %all-gather.20.cloned.1.call-start = ((), (), s32[]{:S(2)}) async-start(), calls=%async_computation.19 | async-start | bytes 2359296 | tf_op jit(solution)/shard_map/all_gather | solution.py:167
  211.3 74.6 %all-gather.16.cloned.1.call-start = ((), (), s32[]{:S(2)}) async-start(), calls=%async_computation.17 | async-start | bytes 2621440 | tf_op jit(solution)/shard_map/all_gather | solution.py:53
  211.8 262.7 %copy-start.32 = (f32[1024]{0:T(1024)}, f32[1024]{0:T(1024)S(1)}, u32[]{:S(2)}) copy-start(f32[1024]{0:T(1024)S(1)} %convert_element_type.167) | copy-start | bytes 12292
  256.9 217.6 %copy-start.42 = (f32[2,128]{1,0:T(2,128)}, f32[2,128]{1,0:T(2,128)S(1)}, u32[]{:S(2)}) copy-start(f32[2,128]{1,0:T(2,128)S(1)} %fusion.57) | copy-start | bytes 3076
  257.9 79.7 %all-gather.18.cloned.1.call-start = ((), (), s32[]{:S(2)}) async-start(), calls=%async_computation.18 | async-start | bytes 2359296 | tf_op jit(solution)/shard_map/all_gather | solution.py:166
  258.4 101.7 %all-gather.24.cloned.1.call-start = ((), (), s32[]{:S(2)}) async-start(), calls=%async_computation.22 | async-start | bytes 2621440 | tf_op jit(solution)/shard_map/all_gather | solution.py:53
  259.2 152.7 %all-gather.22.cloned.1.call-start = ((), (), s32[]{:S(2)}) async-start(), calls=%async_computation.20 | async-start | bytes 2359296 | tf_op jit(solution)/shard_map/all_gather | solution.py:168
  259.9 212.5 %reduce-scatter.20.cloned.1.call-start = ((), (), s32[]{:S(2)}) async-start(), calls=%async_computation.23 | async-start | bytes 5242880 | tf_op jit(solution)/shard_map/reduce_scatter | solution.py:57
  429.2 47.9 %copy-start.41 = (f32[4,512]{1,0:T(4,128)S(1)}, f32[4,512]{1,0:T(4,128)}, u32[]{:S(2)}) copy-start(f32[4,512]{1,0:T(4,128)} %copy-done.40) | copy-start | bytes 24580
  429.3 70.1 %all-gather.26.cloned.1.call-start = ((), (), s32[]{:S(2)}) async-start(), calls=%async_computation.24 | async-start | bytes 2621440 | tf_op jit(solution)/shard_map/all_gather | solution.py:53
  476.9 98.7 %reduce-scatter.24.cloned.1.call-start = ((), (), s32[]{:S(2)}) async-start(), calls=%async_computation.26 | async-start | bytes 1572864 | tf_op jit(solution)/shard_map/reduce_scatter | solution.py:270
  523.7 60.0 %reduce-scatter.22.cloned.1.call-start = ((), (), s32[]{:S(2)}) async-start(), calls=%async_computation.25 | async-start | bytes 1572864 | tf_op jit(solution)/shard_map/reduce_scatter | solution.py:267
  545.3 95.8 %reduce-scatter.40.cloned.1.call-start = ((), (), s32[]{:S(2)}) async-start(), calls=%async_computation.34 | async-start | bytes 2359296
  555.7 153.3 %reduce-scatter.38.cloned.1.call-start = ((), (), s32[]{:S(2)}) async-start(), calls=%async_computation.33 | async-start | bytes 2359296 | tf_op jit(solution)/shard_map/reduce_scatter | solution.py:323
  561.7 217.4 %reduce-scatter.36.cloned.1.call-start = ((), (), s32[]{:S(2)}) async-start(), calls=%async_computation.32 | async-start | bytes 2359296 | tf_op jit(solution)/shard_map/reduce_scatter | solution.py:320
  567.7 275.7 %reduce-scatter.34.cloned.1.call-start = ((), (), s32[]{:S(2)}) async-start(), calls=%async_computation.31 | async-start | bytes 589824 | tf_op jit(solution)/shard_map/reduce_scatter | solution.py:315
  571.0 337.0 %reduce-scatter.32.cloned.1.call-start = ((), (), s32[]{:S(2)}) async-start(), calls=%async_computation.30 | async-start | bytes 589824 | tf_op jit(solution)/shard_map/reduce_scatter | solution.py:312
  578.8 393.9 %reduce-scatter.30.cloned.1.call-start = ((), (), s32[]{:S(2)}) async-start(), calls=%async_computation.29 | async-start | bytes 589824 | tf_op jit(solution)/shard_map/reduce_scatter | solution.py:309
  590.8 447.1 %reduce-scatter.28.cloned.1.call-start = ((), (), s32[]{:S(2)}) async-start(), calls=%async_computation.28 | async-start | bytes 589824 | tf_op jit(solution)/shard_map/reduce_scatter | solution.py:306
  628.7 455.2 %reduce-scatter.26.cloned.1.call-start = ((), (), s32[]{:S(2)}) async-start(), calls=%async_computation.27 | async-start | bytes 5242880 | tf_op jit(solution)/shard_map/reduce_scatter | solution.py:57
  634.2 497.4 %reduce-scatter.18.cloned.1.call-start = ((), (), s32[]{:S(2)}) async-start(), calls=%async_computation.21 | async-start | bytes 5242880 | tf_op jit(solution)/shard_map/reduce_scatter | solution.py:57
  640.9 139.9 %copy-start.52 = (f32[4]{0:T(128)S(1)}, f32[4]{0:T(128)}, u32[]{:S(2)}) copy-start(f32[4]{0:T(128)} %get-tuple-element.202) | copy-start | bytes 52
  640.9 139.9 %copy-start.53 = (f32[4]{0:T(128)S(1)}, f32[4]{0:T(128)}, u32[]{:S(2)}) copy-start(f32[4]{0:T(128)} %get-tuple-element.203) | copy-start | bytes 52
  640.9 442.9 %copy-start.35 = (f32[1024]{0:T(1024)S(1)}, f32[1024]{0:T(1024)}, u32[]{:S(2)}) copy-start(f32[1024]{0:T(1024)} %copy-done.34) | copy-start | bytes 12292
  641.0 442.9 %copy-start.47 = (f32[2,128]{1,0:T(2,128)S(1)}, f32[2,128]{1,0:T(2,128)}, u32[]{:S(2)}) copy-start(f32[2,128]{1,0:T(2,128)} %copy-done.46) | copy-start | bytes 3076
  641.0 444.4 %copy-start.45 = (f32[1024]{0:T(1024)S(1)}, f32[1024]{0:T(1024)}, u32[]{:S(2)}) copy-start(f32[1024]{0:T(1024)} %get-tuple-element.204) | copy-start | bytes 12292
  641.0 484.8 %copy-start.49 = (f32[2,128]{1,0:T(2,128)S(1)}, f32[2,128]{1,0:T(2,128)}, u32[]{:S(2)}) copy-start(f32[2,128]{1,0:T(2,128)} %copy-done.48) | copy-start | bytes 3076
  641.0 490.6 %copy-start.5 = (f32[2,128,1024]{2,1,0:T(8,128)S(1)}, f32[2,128,1024]{2,1,0:T(8,128)}, u32[]{:S(2)}) copy-start(f32[2,128,1024]{2,1,0:T(8,128)} %reduce-scatter.20.cloned.1.call-done) | copy-start | bytes 3145732
  641.0 490.6 %copy-start.33 = (f32[1024]{0:T(1024)S(1)}, f32[1024]{0:T(1024)}, u32[]{:S(2)}) copy-start(f32[1024]{0:T(1024)} %copy-done.32) | copy-start | bytes 12292
  641.0 490.6 %copy-start.43 = (f32[2,128]{1,0:T(2,128)S(1)}, f32[2,128]{1,0:T(2,128)}, u32[]{:S(2)}) copy-start(f32[2,128]{1,0:T(2,128)} %copy-done.42) | copy-start | bytes 3076
  641.0 490.6 %copy-start.51 = (f32[2,128]{1,0:T(2,128)S(1)}, f32[2,128]{1,0:T(2,128)}, u32[]{:S(2)}) copy-start(f32[2,128]{1,0:T(2,128)} %copy-done.50) | copy-start | bytes 3076
  (50 other events, 559.8 us)
Sparse Core Ops, SparseCore 0:
  13.3 25.2 all-gather.9
  142.4 18.7 all-gather.11
  163.3 21.2 all-gather.13
  210.8 44.5 reduce-scatter.15
  429.4 42.9 reduce-scatter.19
  523.8 20.3 reduce-scatter.23
  546.5 20.2 reduce-scatter.21
  570.3 68.4 reduce-scatter.39
  642.4 66.5 reduce-scatter.37
  712.4 66.6 reduce-scatter.35
  782.4 60.9 reduce-scatter.33
  846.9 60.9 reduce-scatter.31
  911.8 60.8 reduce-scatter.29
  976.8 61.0 reduce-scatter.27
  1040.3 43.4 reduce-scatter.25
  1086.3 45.2 reduce-scatter.17
Sparse Core Ops, SparseCore 1:
  213.5 49.3 all-gather.19
  265.0 20.9 all-gather.15
  288.2 49.3 all-gather.17
  339.2 20.9 all-gather.23
  362.5 49.3 all-gather.21
  477.0 22.4 all-gather.25
